TPU v7x, 32 devices: a whole 2x2x4 slice. The times are simulated.
32 devices in a mesh: col: 8 (over z, x), row: 4 (over y, core).
Axes of the slice: x: 2, y: 2, z: 4, core: 2. Of those that a mesh axis runs over, the one named last changes fastest.
Arguments:
- position: float32 [128, 16384], P(None, ('col', 'row')), may hold values from -6 to 6
- momentum: float32 [128, 16384], P(None, ('col', 'row')), may hold values from -6 to 6
- row_factors: bfloat16 [16384, 16, 128], P(('col', 'row')), may hold values from -1 to 1
- col_factors: bfloat16 [16384, 16, 128], P(('col', 'row')), may hold values from -1 to 1
- tile_ranks: int32 [16, 16], replicated, may hold values from 16 to 128, as said below
- log_mean: float32 [16384], P(('col', 'row')), may hold values from -0.5 to 0.5
- counts: int32 [16384], P(('col', 'row')), may hold values from 0 to 11
- step_size: float32 [128], replicated, may hold values from 0.1 to 0.3
Outputs:
- new_position: float32 [128, 16384], P(None, ('col', 'row'))
- new_momentum: float32 [128, 16384], P(None, ('col', 'row'))
- energy_change: float32 [128], replicated
Inputs may be any that keep to these rules, and one draw needn't show every extreme that they name: `tile_ranks`: every entry is a multiple of 16; in every draw some tile has rank 16 and some tile has rank 128.
All inputs are finite; a program needn't handle non-finite values.
Results may differ from a plain program's by a relative error of at most 0.004.
Values may be sent and summed in bfloat16 or wider, within the bound.
A program may use at most 128 MiB of HBM per device.

v0:
```python
import jax
import jax.numpy as jnp
from jax import lax
from jax.sharding import PartitionSpec as P


def partner_2(value, axis, stride):
    mask = 2**stride
    pairs = [(source, source ^ mask) for source in range(lax.axis_size(axis))]
    return lax.ppermute(value, axis, pairs)


def on_device(
    position, momentum, row_factors, col_factors, tile_ranks, log_mean, counts, step_size
):
    chains = position.shape[0]
    tile_count = tile_ranks.shape[0]
    ranked = row_factors.shape[2]
    device = lax.axis_index(("col", "row"))
    own_tile = device // 2
    own_half = device % 2
    levels = jnp.arange(ranked, dtype=jnp.int32)
    col_ranks = lax.dynamic_slice_in_dim(tile_ranks, own_tile, 1, 1)[:, 0]
    row_ranks = lax.dynamic_slice_in_dim(tile_ranks, own_tile, 1, 0)[0]
    col_live = (levels[None, :] < col_ranks[:, None]).astype(jnp.float32)[:, :, None]
    row_live = (levels[None, :] < row_ranks[:, None]).astype(jnp.float32)[:, :, None]
    rate_base = counts.astype(jnp.float32)[None, :]

    def deliver(partial_value):
        halved = partial_value.reshape(2 * tile_count, ranked // 2, chains)
        arrived = lax.all_to_all(halved, ("col", "row"), split_axis=0, concat_axis=0, tiled=True)
        summed = arrived.reshape(tile_count, 2, ranked // 2, chains).astype(jnp.float32).sum(axis=1)
        summed = summed.astype(jnp.bfloat16)
        partner = partner_2(summed, "row", 0)
        lower_first = jnp.concatenate([summed, partner], axis=1)
        upper_first = jnp.concatenate([partner, summed], axis=1)
        return jnp.where(own_half == 0, lower_first, upper_first)

    def gradient(values):
        rounded = values.astype(jnp.bfloat16)
        partial_value = jnp.einsum(
            "yik,hy->ikh", col_factors, rounded, preferred_element_type=jnp.float32
        )
        partial_value = (partial_value * col_live).astype(jnp.bfloat16)
        coefficient = deliver(partial_value)
        latent_field = jnp.einsum(
            "xjk,jkh->hx", row_factors, coefficient, preferred_element_type=jnp.float32
        )
        exponent = log_mean[None, :] + latent_field
        intensity = jnp.exp(exponent)
        residual = rate_base - intensity
        adjoint = jnp.einsum(
            "xjk,hx->jkh",
            row_factors,
            residual.astype(jnp.bfloat16),
            preferred_element_type=jnp.float32,
        )
        adjoint = (adjoint * row_live).astype(jnp.bfloat16)
        returned = deliver(adjoint)
        pulled = jnp.einsum(
            "yik,ikh->hy", col_factors, returned, preferred_element_type=jnp.float32
        )
        energy = jnp.sum(intensity - rate_base * exponent + 0.5 * values * values, axis=1)
        return (values - pulled, energy)

    full_step = step_size[:, None]

    def leapfrog(section, carry):
        shifted, moment, start_energy, end_energy = carry
        forces, energy = gradient(shifted)
        weight = jnp.where(section == 1, 1.0, 0.5).astype(jnp.float32)
        moment = moment - weight * full_step * forces
        advance = jnp.where(section < 2, full_step * moment, jnp.zeros_like(moment))
        shifted = shifted + advance
        start_energy = jnp.where(section == 0, energy, start_energy)
        end_energy = jnp.where(section == 2, energy, end_energy)
        return (shifted, moment, start_energy, end_energy)

    empty = jnp.zeros((chains,), jnp.float32)
    shifted, moment, start_energy, end_energy = lax.fori_loop(
        0, 3, leapfrog, (position, momentum, empty, empty)
    )
    kinetic = 0.5 * jnp.sum(moment * moment - momentum * momentum, axis=1)
    change = lax.psum(end_energy - start_energy + kinetic, ("col", "row"))
    return (shifted, moment, change)


def solution(mesh):
    in_specs = (
        P(None, ("col", "row")),
        P(None, ("col", "row")),
        P(("col", "row"), None, None),
        P(("col", "row"), None, None),
        P(),
        P(("col", "row")),
        P(("col", "row")),
        P(),
    )
    out_specs = (P(None, ("col", "row")), P(None, ("col", "row")), P())
    return jax.shard_map(
        on_device, mesh=mesh, in_specs=in_specs, out_specs=out_specs, check_vma=False
    )
```

profile of v0, /device:TPU:0, one launch (start us, length us, event | category | flops | bytes accessed | tf_op | source)
XLA Modules:
  0.0 186.0 jit_solution(8267048132765236905)
XLA Ops:
  0.6 0.0 copy-start
  0.7 0.7 copy-done
  1.3 0.2 dynamic-slice_reduce_fusion
  1.5 2.1 %copy.23 = bf16[512,16,128]{2,0,1:T(8,128)(2,1)S(1)} copy(bf16[512,16,128]{2,1,0:T(8,128)(2,1)} %param.13) | data formatting | bytes 4194304
  3.7 0.0 copy-start.7
  3.7 0.0 copy-start.3
  3.7 0.0 copy-start.6
  3.7 0.0 copy-start.8
  3.7 0.0 copy-start.9
  3.7 4.4 %copy.24 = bf16[512,16,128]{0,2,1:T(8,128)(2,1)} copy(bf16[512,16,128]{2,1,0:T(8,128)(2,1)} %param.12) | data formatting | bytes 4194304
  8.1 0.0 copy-done.3
  8.1 0.0 copy-done.6
  8.1 0.0 copy-done.8
  8.2 0.0 copy-start.4
  8.2 138.8 %while.23 = (s32[]{:T(128)}, f32[128,512]{1,0:T(8,128)S(1)}, f32[128,512]{1,0:T(8,128)S(1)}, f32[128]{0:T(128)S(1)}, f32[128]{0:T(128)S(1)}, /*index=5*/f32[128,...) while((s32[]{:T(128)}, f32[128,512]{1,0:T(8,128)S(1)}, ...), condition=%wide.region_4.5_spmd.clone, body=%wide.region_0.4_spmd.clone.sunk | while | flops 1080828416 | bytes 28880336 | solution.py:80
  8.2 0.1 convert_bitcast_fusion.4
  8.3 0.9 fusion.47
  9.2 22.7 %all_to_all.30 = bf16[32,64,128]{2,1,0:T(8,128)(2,1)S(1)} all-to-all(bf16[32,64,128]{2,1,0:T(8,128)(2,1)S(1)} %bitcast.77), channel_id=1, replica_groups=mesh['col'=8,'row'=4] {'col','row'}, dimensions={0} | all-to-all | bytes 1048576 | tf_op jit(solution)/shard_map/while/body/eval_jaxpr/all_to_all | solution.py:31
  31.9 0.1 bitcast_reduce_fusion.4
  32.0 0.1 collective-permute-start
  32.1 0.1 convert_bitcast_fusion.5
  32.1 1.4 collective-permute-done
  33.6 0.5 fusion.48
  34.1 0.7 fusion.49
  34.8 0.3 multiply_convert_fusion.2
  35.1 18.4 %all_to_all.31 = bf16[32,64,128]{2,1,0:T(8,128)(2,1)S(1)} all-to-all(bf16[32,64,128]{2,1,0:T(8,128)(2,1)S(1)} %bitcast.76), channel_id=1, replica_groups=mesh['col'=8,'row'=4] {'col','row'}, dimensions={0} | all-to-all | bytes 1048576 | tf_op jit(solution)/shard_map/while/body/eval_jaxpr/all_to_all | solution.py:31
  53.5 0.1 bitcast_reduce_fusion.5
  53.6 0.1 collective-permute-start.1
  53.7 1.6 collective-permute-done.1
  55.4 2.0 %fusion.50 = (f32[128]{0:T(128)S(1)}, f32[128,512]{1,0:T(8,128)S(1)}, f32[128,512]{1,0:T(8,128)S(1)}) fusion(f32[128,512]{1,0:T(8,128)S(1)} %get-tuple-element.580, f32[128,512]{1,0:T(8,128)S(1)} %fusion.48, f32[512]{0:T(512)S(1)} %bitcast.80, f32[128]{0:T(128)S(1)} %bitcast.82, pred[]{:T(512)S(6)} %lt.137, f32[128,512]{1,0:T(8,128)S(1)} %get-tuple-element.581, ...), kind=kOutput, calls=%fused_computation.29.clone.1 | convolution fusion | flops 271581056 | bytes 3935746 | tf_op jit(solution)/shard_map/while/body/eval_jaxpr/yik,ikh->hy/dot_general | solution.py:60
  57.4 0.1 convert_bitcast_fusion.4
  57.4 0.9 fusion.47
  58.3 18.4 %all_to_all.30 = bf16[32,64,128]{2,1,0:T(8,128)(2,1)S(1)} all-to-all(bf16[32,64,128]{2,1,0:T(8,128)(2,1)S(1)} %bitcast.77), channel_id=1, replica_groups=mesh['col'=8,'row'=4] {'col','row'}, dimensions={0} | all-to-all | bytes 1048576 | tf_op jit(solution)/shard_map/while/body/eval_jaxpr/all_to_all | solution.py:31
  76.7 0.1 bitcast_reduce_fusion.4
  76.8 0.1 collective-permute-start
  76.9 0.1 convert_bitcast_fusion.5
  77.0 1.4 collective-permute-done
  78.4 0.5 fusion.48
  78.9 0.7 fusion.49
  79.6 0.3 multiply_convert_fusion.2
  80.0 18.4 %all_to_all.31 = bf16[32,64,128]{2,1,0:T(8,128)(2,1)S(1)} all-to-all(bf16[32,64,128]{2,1,0:T(8,128)(2,1)S(1)} %bitcast.76), channel_id=1, replica_groups=mesh['col'=8,'row'=4] {'col','row'}, dimensions={0} | all-to-all | bytes 1048576 | tf_op jit(solution)/shard_map/while/body/eval_jaxpr/all_to_all | solution.py:31
  98.4 0.1 bitcast_reduce_fusion.5
  98.4 0.1 collective-permute-start.1
  98.5 1.6 collective-permute-done.1
  100.2 1.9 %fusion.50 = (f32[128]{0:T(128)S(1)}, f32[128,512]{1,0:T(8,128)S(1)}, f32[128,512]{1,0:T(8,128)S(1)}) fusion(f32[128,512]{1,0:T(8,128)S(1)} %get-tuple-element.580, f32[128,512]{1,0:T(8,128)S(1)} %fusion.48, f32[512]{0:T(512)S(1)} %bitcast.80, f32[128]{0:T(128)S(1)} %bitcast.82, pred[]{:T(512)S(6)} %lt.137, f32[128,512]{1,0:T(8,128)S(1)} %get-tuple-element.581, ...), kind=kOutput, calls=%fused_computation.29.clone.1 | convolution fusion | flops 271581056 | bytes 3935746 | tf_op jit(solution)/shard_map/while/body/eval_jaxpr/yik,ikh->hy/dot_general | solution.py:60
  102.2 0.1 convert_bitcast_fusion.4
  102.2 0.9 fusion.47
  103.2 18.4 %all_to_all.30 = bf16[32,64,128]{2,1,0:T(8,128)(2,1)S(1)} all-to-all(bf16[32,64,128]{2,1,0:T(8,128)(2,1)S(1)} %bitcast.77), channel_id=1, replica_groups=mesh['col'=8,'row'=4] {'col','row'}, dimensions={0} | all-to-all | bytes 1048576 | tf_op jit(solution)/shard_map/while/body/eval_jaxpr/all_to_all | solution.py:31
  121.6 0.1 bitcast_reduce_fusion.4
  121.6 0.1 collective-permute-start
  121.7 0.1 convert_bitcast_fusion.5
  121.8 1.4 collective-permute-done
  123.2 0.5 fusion.48
  123.7 0.7 fusion.49
  124.4 0.3 multiply_convert_fusion.2
  124.8 18.4 %all_to_all.31 = bf16[32,64,128]{2,1,0:T(8,128)(2,1)S(1)} all-to-all(bf16[32,64,128]{2,1,0:T(8,128)(2,1)S(1)} %bitcast.76), channel_id=1, replica_groups=mesh['col'=8,'row'=4] {'col','row'}, dimensions={0} | all-to-all | bytes 1048576 | tf_op jit(solution)/shard_map/while/body/eval_jaxpr/all_to_all | solution.py:31
  143.2 0.1 bitcast_reduce_fusion.5
  143.3 0.1 collective-permute-start.1
  143.4 1.6 collective-permute-done.1
  145.0 2.0 %fusion.50 = (f32[128]{0:T(128)S(1)}, f32[128,512]{1,0:T(8,128)S(1)}, f32[128,512]{1,0:T(8,128)S(1)}) fusion(f32[128,512]{1,0:T(8,128)S(1)} %get-tuple-element.580, f32[128,512]{1,0:T(8,128)S(1)} %fusion.48, f32[512]{0:T(512)S(1)} %bitcast.80, f32[128]{0:T(128)S(1)} %bitcast.82, pred[]{:T(512)S(6)} %lt.137, f32[128,512]{1,0:T(8,128)S(1)} %get-tuple-element.581, ...), kind=kOutput, calls=%fused_computation.29.clone.1 | convolution fusion | flops 271581056 | bytes 3935746 | tf_op jit(solution)/shard_map/while/body/eval_jaxpr/yik,ikh->hy/dot_general | solution.py:60
  147.0 0.0 copy-start.2
  147.0 0.0 copy-start.5
  147.0 0.1 subtract_reduce_fusion
  147.1 38.9 %psum.7 = f32[128]{0:T(128)} all-reduce(f32[128]{0:T(128)S(1)} %multiply_add_fusion), channel_id=1, replica_groups=mesh['col'=8,'row'=4] {'col','row'}, use_global_device_ids=true, to_apply=%region_6.7 | all-reduce | flops 128 | bytes 1024 | tf_op jit(solution)/shard_map/psum | solution.py:84
  (22 shorter events, 0.1 us)
Async XLA Ops:
  0.6 0.7 copy-start
  3.7 4.4 %copy-start.7 = (s32[512]{0:T(512)S(1)}, s32[512]{0:T(512)}, u32[]{:S(2)}) copy-start(s32[512]{0:T(512)} %param.16) | copy-start | bytes 6148
  3.7 4.4 %copy-start.3 = (f32[128,512]{1,0:T(8,128)S(1)}, f32[128,512]{1,0:T(8,128)}, u32[]{:S(2)}) copy-start(f32[128,512]{1,0:T(8,128)} %param.10) | copy-start | bytes 786436
  3.7 4.4 %copy-start.6 = (f32[128,512]{1,0:T(8,128)S(1)}, f32[128,512]{1,0:T(8,128)}, u32[]{:S(2)}) copy-start(f32[128,512]{1,0:T(8,128)} %param.11) | copy-start | bytes 786436
  3.7 4.4 %copy-start.8 = (f32[512]{0:T(512)S(1)}, f32[512]{0:T(512)}, u32[]{:S(2)}) copy-start(f32[512]{0:T(512)} %param.15) | copy-start | bytes 6148
  3.7 4.4 %copy-start.9 = (f32[128]{0:T(128)S(1)}, f32[128]{0:T(128)}, u32[]{:S(2)}) copy-start(f32[128]{0:T(128)} %param.17) | copy-start | bytes 1540
  8.2 138.9 %copy-start.4 = (f32[128,512]{1,0:T(8,128)S(1)}, f32[128,512]{1,0:T(8,128)}, u32[]{:S(2)}) copy-start(f32[128,512]{1,0:T(8,128)} %param.11) | copy-start | bytes 786436
  8.3 25.4 %copy-start.1 = (bf16[512,16,128]{0,2,1:T(8,128)(2,1)S(1)}, bf16[512,16,128]{0,2,1:T(8,128)(2,1)}, u32[]{:S(2)}) copy-start(bf16[512,16,128]{0,2,1:T(8,128)(2,1)} %get-tuple-element.607) | copy-start | bytes 6291460 | tf_op jit(solution)/shard_map/while
  32.0 1.6 collective-permute-start
  53.6 1.7 collective-permute-start.1
  57.4 21.0 %copy-start.1 = (bf16[512,16,128]{0,2,1:T(8,128)(2,1)S(1)}, bf16[512,16,128]{0,2,1:T(8,128)(2,1)}, u32[]{:S(2)}) copy-start(bf16[512,16,128]{0,2,1:T(8,128)(2,1)} %get-tuple-element.607) | copy-start | bytes 6291460 | tf_op jit(solution)/shard_map/while
  76.8 1.6 collective-permute-start
  98.4 1.7 collective-permute-start.1
  102.2 21.0 %copy-start.1 = (bf16[512,16,128]{0,2,1:T(8,128)(2,1)S(1)}, bf16[512,16,128]{0,2,1:T(8,128)(2,1)}, u32[]{:S(2)}) copy-start(bf16[512,16,128]{0,2,1:T(8,128)(2,1)} %get-tuple-element.607) | copy-start | bytes 6291460 | tf_op jit(solution)/shard_map/while
  121.6 1.6 collective-permute-start
  143.3 1.7 collective-permute-start.1
  147.0 39.1 %copy-start.2 = (f32[128,512]{1,0:T(8,128)}, f32[128,512]{1,0:T(8,128)S(1)}, u32[]{:S(2)}) copy-start(f32[128,512]{1,0:T(8,128)S(1)} %get-tuple-element.347) | copy-start | bytes 786436
  147.0 39.0 %copy-start.5 = (f32[128,512]{1,0:T(8,128)}, f32[128,512]{1,0:T(8,128)S(1)}, u32[]{:S(2)}) copy-start(f32[128,512]{1,0:T(8,128)S(1)} %get-tuple-element.348) | copy-start | bytes 786436
where the time goes:
time: 187 us; the launch traced here: 186 us
  blocking collectives  154 us (82%)
  matrix products  12.1 us (6%)
  waiting for transfers between devices  9.24 us (5%)
  local copies, waits for them, and re-layouts  7.44 us (4%)
  other arithmetic  2.09 us (1%)
    all_to_all x6, blocking collectives, deliver(): lax.all_to_all(halved, ('col', 'row'), split_axis=0, concat_axis=0, tiled...  115 us
    psum x1, blocking collectives, on_device(): change = lax.psum(end_energy - start_energy + kinetic, ('col', 'row'))  38.9 us
    ppermute x6, waiting for transfers between devices, partner_2(): return lax.ppermute(value, axis, pairs)  9.24 us
    unnamed x20, local copies, waits for them, and re-layouts  7.24 us
    dot_general x3, matrix products, gradient(): jnp.einsum('yik,ikh->hy', col_factors, returned, preferred_element_type=j...  5.85 us
  transfers between devices with their start and end apart: 6, of which 6 were waited for; matrix products, arithmetic and copies ran while one was open for 0% of the time, Pallas kernels for 0%

commit v1 on v0

--- a/solution.py
+++ b/solution.py
@@ -81,7 +81,9 @@
         0, 3, leapfrog, (position, momentum, empty, empty)
     )
     kinetic = 0.5 * jnp.sum(moment * moment - momentum * momentum, axis=1)
-    change = lax.psum(end_energy - start_energy + kinetic, ("col", "row"))
+    block_in = end_energy - start_energy + kinetic
+    reached = jax.lax.psum(block_in, axis_name="row")
+    change = jax.lax.psum(reached, axis_name="col")
     return (shifted, moment, change)
 
 

time: 187 us -> 174 us (0.930)
  blocking collectives: 154 us -> 141 us
    psum x1 -> x2, blocking collectives: 38.9 us -> 26.2 us  [the longest x1 19.7 us: on_device(): change = jax.lax.psum(reached, axis_name='col')]
where the time goes in v1:
time: 174 us; the launch traced here: 173 us
  blocking collectives  141 us (81%)
  matrix products  12.1 us (7%)
  waiting for transfers between devices  9.24 us (5%)
  local copies, waits for them, and re-layouts  7.44 us (4%)
  other arithmetic  2.09 us (1%)
    all_to_all x6, blocking collectives, deliver(): lax.all_to_all(halved, ('col', 'row'), split_axis=0, concat_axis=0, tiled...  115 us
    psum x1, blocking collectives, on_device(): change = jax.lax.psum(reached, axis_name='col')  19.7 us
    ppermute x6, waiting for transfers between devices, partner_2(): return lax.ppermute(value, axis, pairs)  9.24 us
    unnamed x20, local copies, waits for them, and re-layouts  7.24 us
    psum x1, blocking collectives, on_device(): reached = jax.lax.psum(block_in, axis_name='row')  6.48 us
    dot_general x3, matrix products, gradient(): jnp.einsum('yik,ikh->hy', col_factors, returned, preferred_element_type=j...  5.85 us
  transfers between devices with their start and end apart: 6, of which 6 were waited for; matrix products, arithmetic and copies ran while one was open for 0% of the time, Pallas kernels for 0%

profile of v1, /device:TPU:0, one launch (start us, length us, event | category | flops | bytes accessed | tf_op | source)
XLA Modules:
  0.0 173.3 jit_solution(7452111277951621848)
XLA Ops:
  0.6 0.0 copy-start
  0.7 0.7 copy-done
  1.3 0.2 dynamic-slice_reduce_fusion
  1.5 2.1 %copy.23 = bf16[512,16,128]{2,0,1:T(8,128)(2,1)S(1)} copy(bf16[512,16,128]{2,1,0:T(8,128)(2,1)} %param.13) | data formatting | bytes 4194304
  3.7 0.0 copy-start.7
  3.7 0.0 copy-start.3
  3.7 0.0 copy-start.6
  3.7 0.0 copy-start.8
  3.7 0.0 copy-start.9
  3.7 4.4 %copy.24 = bf16[512,16,128]{0,2,1:T(8,128)(2,1)} copy(bf16[512,16,128]{2,1,0:T(8,128)(2,1)} %param.12) | data formatting | bytes 4194304
  8.1 0.0 copy-done.3
  8.1 0.0 copy-done.6
  8.2 0.0 copy-start.4
  8.2 138.8 %while.23 = (s32[]{:T(128)}, f32[128,512]{1,0:T(8,128)S(1)}, f32[128,512]{1,0:T(8,128)S(1)}, f32[128]{0:T(128)S(1)}, f32[128]{0:T(128)S(1)}, /*index=5*/f32[128,...) while((s32[]{:T(128)}, f32[128,512]{1,0:T(8,128)S(1)}, ...), condition=%wide.region_4.5_spmd.clone, body=%wide.region_0.4_spmd.clone.sunk | while | flops 1080828416 | bytes 28880336 | solution.py:80
  8.2 0.1 convert_bitcast_fusion.4
  8.3 0.9 fusion.47
  9.2 22.7 %all_to_all.30 = bf16[32,64,128]{2,1,0:T(8,128)(2,1)S(1)} all-to-all(bf16[32,64,128]{2,1,0:T(8,128)(2,1)S(1)} %bitcast.77), channel_id=1, replica_groups=mesh['col'=8,'row'=4] {'col','row'}, dimensions={0} | all-to-all | bytes 1048576 | tf_op jit(solution)/shard_map/while/body/eval_jaxpr/all_to_all | solution.py:31
  31.9 0.1 bitcast_reduce_fusion.4
  32.0 0.1 collective-permute-start
  32.1 0.1 convert_bitcast_fusion.5
  32.1 1.4 collective-permute-done
  33.6 0.5 fusion.48
  34.1 0.7 fusion.49
  34.8 0.3 multiply_convert_fusion.2
  35.1 18.4 %all_to_all.31 = bf16[32,64,128]{2,1,0:T(8,128)(2,1)S(1)} all-to-all(bf16[32,64,128]{2,1,0:T(8,128)(2,1)S(1)} %bitcast.76), channel_id=1, replica_groups=mesh['col'=8,'row'=4] {'col','row'}, dimensions={0} | all-to-all | bytes 1048576 | tf_op jit(solution)/shard_map/while/body/eval_jaxpr/all_to_all | solution.py:31
  53.5 0.1 bitcast_reduce_fusion.5
  53.6 0.1 collective-permute-start.1
  53.7 1.6 collective-permute-done.1
  55.4 2.0 %fusion.50 = (f32[128]{0:T(128)S(1)}, f32[128,512]{1,0:T(8,128)S(1)}, f32[128,512]{1,0:T(8,128)S(1)}) fusion(f32[128,512]{1,0:T(8,128)S(1)} %get-tuple-element.580, f32[128,512]{1,0:T(8,128)S(1)} %fusion.48, f32[512]{0:T(512)S(1)} %bitcast.80, f32[128]{0:T(128)S(1)} %bitcast.82, pred[]{:T(512)S(6)} %lt.137, f32[128,512]{1,0:T(8,128)S(1)} %get-tuple-element.581, ...), kind=kOutput, calls=%fused_computation.29.clone.1 | convolution fusion | flops 271581056 | bytes 3935746 | tf_op jit(solution)/shard_map/while/body/eval_jaxpr/yik,ikh->hy/dot_general | solution.py:60
  57.4 0.1 convert_bitcast_fusion.4
  57.4 0.9 fusion.47
  58.3 18.4 %all_to_all.30 = bf16[32,64,128]{2,1,0:T(8,128)(2,1)S(1)} all-to-all(bf16[32,64,128]{2,1,0:T(8,128)(2,1)S(1)} %bitcast.77), channel_id=1, replica_groups=mesh['col'=8,'row'=4] {'col','row'}, dimensions={0} | all-to-all | bytes 1048576 | tf_op jit(solution)/shard_map/while/body/eval_jaxpr/all_to_all | solution.py:31
  76.7 0.1 bitcast_reduce_fusion.4
  76.8 0.1 collective-permute-start
  76.9 0.1 convert_bitcast_fusion.5
  77.0 1.4 collective-permute-done
  78.4 0.5 fusion.48
  78.9 0.7 fusion.49
  79.6 0.3 multiply_convert_fusion.2
  80.0 18.4 %all_to_all.31 = bf16[32,64,128]{2,1,0:T(8,128)(2,1)S(1)} all-to-all(bf16[32,64,128]{2,1,0:T(8,128)(2,1)S(1)} %bitcast.76), channel_id=1, replica_groups=mesh['col'=8,'row'=4] {'col','row'}, dimensions={0} | all-to-all | bytes 1048576 | tf_op jit(solution)/shard_map/while/body/eval_jaxpr/all_to_all | solution.py:31
  98.4 0.1 bitcast_reduce_fusion.5
  98.4 0.1 collective-permute-start.1
  98.5 1.6 collective-permute-done.1
  100.2 1.9 %fusion.50 = (f32[128]{0:T(128)S(1)}, f32[128,512]{1,0:T(8,128)S(1)}, f32[128,512]{1,0:T(8,128)S(1)}) fusion(f32[128,512]{1,0:T(8,128)S(1)} %get-tuple-element.580, f32[128,512]{1,0:T(8,128)S(1)} %fusion.48, f32[512]{0:T(512)S(1)} %bitcast.80, f32[128]{0:T(128)S(1)} %bitcast.82, pred[]{:T(512)S(6)} %lt.137, f32[128,512]{1,0:T(8,128)S(1)} %get-tuple-element.581, ...), kind=kOutput, calls=%fused_computation.29.clone.1 | convolution fusion | flops 271581056 | bytes 3935746 | tf_op jit(solution)/shard_map/while/body/eval_jaxpr/yik,ikh->hy/dot_general | solution.py:60
  102.2 0.1 convert_bitcast_fusion.4
  102.2 0.9 fusion.47
  103.2 18.4 %all_to_all.30 = bf16[32,64,128]{2,1,0:T(8,128)(2,1)S(1)} all-to-all(bf16[32,64,128]{2,1,0:T(8,128)(2,1)S(1)} %bitcast.77), channel_id=1, replica_groups=mesh['col'=8,'row'=4] {'col','row'}, dimensions={0} | all-to-all | bytes 1048576 | tf_op jit(solution)/shard_map/while/body/eval_jaxpr/all_to_all | solution.py:31
  121.6 0.1 bitcast_reduce_fusion.4
  121.6 0.1 collective-permute-start
  121.7 0.1 convert_bitcast_fusion.5
  121.8 1.4 collective-permute-done
  123.2 0.5 fusion.48
  123.7 0.7 fusion.49
  124.4 0.3 multiply_convert_fusion.2
  124.8 18.4 %all_to_all.31 = bf16[32,64,128]{2,1,0:T(8,128)(2,1)S(1)} all-to-all(bf16[32,64,128]{2,1,0:T(8,128)(2,1)S(1)} %bitcast.76), channel_id=1, replica_groups=mesh['col'=8,'row'=4] {'col','row'}, dimensions={0} | all-to-all | bytes 1048576 | tf_op jit(solution)/shard_map/while/body/eval_jaxpr/all_to_all | solution.py:31
  143.2 0.1 bitcast_reduce_fusion.5
  143.3 0.1 collective-permute-start.1
  143.4 1.6 collective-permute-done.1
  145.0 2.0 %fusion.50 = (f32[128]{0:T(128)S(1)}, f32[128,512]{1,0:T(8,128)S(1)}, f32[128,512]{1,0:T(8,128)S(1)}) fusion(f32[128,512]{1,0:T(8,128)S(1)} %get-tuple-element.580, f32[128,512]{1,0:T(8,128)S(1)} %fusion.48, f32[512]{0:T(512)S(1)} %bitcast.80, f32[128]{0:T(128)S(1)} %bitcast.82, pred[]{:T(512)S(6)} %lt.137, f32[128,512]{1,0:T(8,128)S(1)} %get-tuple-element.581, ...), kind=kOutput, calls=%fused_computation.29.clone.1 | convolution fusion | flops 271581056 | bytes 3935746 | tf_op jit(solution)/shard_map/while/body/eval_jaxpr/yik,ikh->hy/dot_general | solution.py:60
  147.0 0.0 copy-start.2
  147.0 0.0 copy-start.5
  147.0 0.1 subtract_reduce_fusion
  147.1 6.5 %psum.14 = f32[128]{0:T(128)S(1)} all-reduce(f32[128]{0:T(128)S(1)} %multiply_add_fusion), channel_id=1, replica_groups=mesh['col'=8,'row'=4] {'row'}, use_global_device_ids=true, to_apply=%region_6.7 | all-reduce | flops 128 | bytes 1024 | tf_op jit(solution)/shard_map/psum | solution.py:85
  153.6 19.7 %psum.15 = f32[128]{0:T(128)} all-reduce(f32[128]{0:T(128)S(1)} %psum.14), channel_id=1, replica_groups=mesh['col'=8,'row'=4] {'col'}, use_global_device_ids=true, to_apply=%region_7.8 | all-reduce | flops 128 | bytes 1024 | tf_op jit(solution)/shard_map/psum | solution.py:86
  (23 shorter events, 0.1 us)
Async XLA Ops:
  0.6 0.7 copy-start
  3.7 4.4 %copy-start.7 = (s32[512]{0:T(512)S(1)}, s32[512]{0:T(512)}, u32[]{:S(2)}) copy-start(s32[512]{0:T(512)} %param.16) | copy-start | bytes 6148
  3.7 4.4 %copy-start.3 = (f32[128,512]{1,0:T(8,128)S(1)}, f32[128,512]{1,0:T(8,128)}, u32[]{:S(2)}) copy-start(f32[128,512]{1,0:T(8,128)} %param.10) | copy-start | bytes 786436
  3.7 4.4 %copy-start.6 = (f32[128,512]{1,0:T(8,128)S(1)}, f32[128,512]{1,0:T(8,128)}, u32[]{:S(2)}) copy-start(f32[128,512]{1,0:T(8,128)} %param.11) | copy-start | bytes 786436
  3.7 4.4 %copy-start.8 = (f32[512]{0:T(512)S(1)}, f32[512]{0:T(512)}, u32[]{:S(2)}) copy-start(f32[512]{0:T(512)} %param.15) | copy-start | bytes 6148
  3.7 4.4 %copy-start.9 = (f32[128]{0:T(128)S(1)}, f32[128]{0:T(128)}, u32[]{:S(2)}) copy-start(f32[128]{0:T(128)} %param.17) | copy-start | bytes 1540
  8.2 138.9 %copy-start.4 = (f32[128,512]{1,0:T(8,128)S(1)}, f32[128,512]{1,0:T(8,128)}, u32[]{:S(2)}) copy-start(f32[128,512]{1,0:T(8,128)} %param.11) | copy-start | bytes 786436
  8.3 25.4 %copy-start.1 = (bf16[512,16,128]{0,2,1:T(8,128)(2,1)S(1)}, bf16[512,16,128]{0,2,1:T(8,128)(2,1)}, u32[]{:S(2)}) copy-start(bf16[512,16,128]{0,2,1:T(8,128)(2,1)} %get-tuple-element.607) | copy-start | bytes 6291460 | tf_op jit(solution)/shard_map/while
  32.0 1.6 collective-permute-start
  53.6 1.7 collective-permute-start.1
  57.4 21.0 %copy-start.1 = (bf16[512,16,128]{0,2,1:T(8,128)(2,1)S(1)}, bf16[512,16,128]{0,2,1:T(8,128)(2,1)}, u32[]{:S(2)}) copy-start(bf16[512,16,128]{0,2,1:T(8,128)(2,1)} %get-tuple-element.607) | copy-start | bytes 6291460 | tf_op jit(solution)/shard_map/while
  76.8 1.6 collective-permute-start
  98.4 1.7 collective-permute-start.1
  102.2 21.0 %copy-start.1 = (bf16[512,16,128]{0,2,1:T(8,128)(2,1)S(1)}, bf16[512,16,128]{0,2,1:T(8,128)(2,1)}, u32[]{:S(2)}) copy-start(bf16[512,16,128]{0,2,1:T(8,128)(2,1)} %get-tuple-element.607) | copy-start | bytes 6291460 | tf_op jit(solution)/shard_map/while
  121.6 1.6 collective-permute-start
  143.3 1.7 collective-permute-start.1
  147.0 26.3 %copy-start.2 = (f32[128,512]{1,0:T(8,128)}, f32[128,512]{1,0:T(8,128)S(1)}, u32[]{:S(2)}) copy-start(f32[128,512]{1,0:T(8,128)S(1)} %get-tuple-element.347) | copy-start | bytes 786436
  147.0 26.3 %copy-start.5 = (f32[128,512]{1,0:T(8,128)}, f32[128,512]{1,0:T(8,128)S(1)}, u32[]{:S(2)}) copy-start(f32[128,512]{1,0:T(8,128)S(1)} %get-tuple-element.348) | copy-start | bytes 786436
